TPU v7x, 32 devices: a whole 2x2x4 slice. The times are simulated.
32 devices in a mesh: row: 4 (over z), col: 8 (over y, x, core).
Axes of the slice: x: 2, y: 2, z: 4, core: 2. Of those that a mesh axis runs over, the one named last changes fastest.
Arguments:
- amplitudes: bfloat16 [16, 16, 12, 4096], P('row', 'col'), may hold values from -6 to 6
- integrals: bfloat16 [16, 16, 47, 4096], P('row', 'col'), may hold values from -0.1875 to 0.1875
- pair_lists: int32 [4, 12, 2], replicated, may hold values from 0 to 46, as said below
- tile_counts: int32 [4], replicated, may hold values from 1 to 12, as said below
Outputs:
- symmetric: float32 [16, 16, 12, 4096], P('row', 'col')
Inputs may be any that keep to these rules, and one draw needn't show every extreme that they name: `pair_lists`: each grid row lists 12 distinct ordered pairs of different tiles. `tile_counts`: the largest count equals 12.
All inputs are finite; a program needn't handle non-finite values.
Results may differ from a plain program's by a relative error of at most 0.0029.
Values may be sent and summed in bfloat16 or wider, within the bound.
No kernel may reach another device: no remote copies, remote signals or barrier semaphores. Data moves between devices by JAX's collectives and lax.ppermute only.
A program may use at most 128 MiB of HBM per device.

v0:
```python
import jax
import jax.numpy as jnp
from jax import lax
from jax.sharding import PartitionSpec as P

TILE = 64


def mirror_pairs(row_devices, col_devices, step):
    ratio = col_devices // row_devices
    pairs = []
    for row in range(row_devices):
        for col in range(col_devices):
            part = (col % ratio + step) % ratio
            pairs.append((row * col_devices + col, col // ratio * col_devices + row * ratio + part))
    return pairs


def on_device(amplitudes, integrals, pair_lists, tile_counts):
    occ_row, occ_col, slot_count, square = amplitudes.shape
    tile_width = TILE
    row_devices = lax.axis_size("row")
    col_devices = lax.axis_size("col")
    col_ratio = col_devices // row_devices
    my_row = lax.axis_index("row")
    my_col = lax.axis_index("col")
    partner_row = my_col // col_ratio
    tile_first = pair_lists[:, :, 0]
    tile_second = pair_lists[:, :, 1]
    packed = jnp.take(integrals, tile_second.reshape(-1), axis=2)
    packed = packed.reshape(occ_row, occ_col, row_devices, slot_count, square)
    received = lax.all_to_all(packed, "row", split_axis=2, concat_axis=0, tiled=True)
    received = received.reshape(occ_row * row_devices, occ_col, slot_count, square)
    piece = lax.all_gather(amplitudes, "col", axis=1, tiled=True)
    piece_count = piece.shape[1]
    left_tiles = piece.reshape(occ_row, piece_count, slot_count, tile_width, tile_width)
    right_tiles = received.reshape(piece_count, occ_col, slot_count, tile_width, tile_width)
    cycle_sum = jnp.einsum(
        "iksac,kjscb->ijsab", left_tiles, right_tiles, preferred_element_type=jnp.float32
    )
    my_count = lax.dynamic_index_in_dim(tile_counts, my_row, 0, keepdims=False)
    live_slots = (jnp.arange(slot_count, dtype=jnp.int32) < my_count).astype(jnp.float32)
    cycle_value = (cycle_sum * live_slots[None, None, :, None, None]).astype(jnp.bfloat16)
    cycle = cycle_value.reshape(occ_row, occ_col, slot_count, square)
    halves = cycle.reshape(col_ratio, occ_col, occ_col, slot_count, square)
    col_part = lax.rem(my_col, col_ratio)
    arrived = []
    for step in range(col_ratio):
        part = lax.rem(col_part + step, col_ratio)
        block = lax.dynamic_index_in_dim(halves, part, 0, keepdims=False)
        arrived.append(
            lax.ppermute(block, ("row", "col"), mirror_pairs(row_devices, col_devices, step))
        )
    arrived = jnp.stack(arrived)
    order = lax.rem(col_part - jnp.arange(col_ratio) + col_ratio, col_ratio)
    arrived = jnp.take(arrived, order, axis=0)
    mirror_block = jnp.moveaxis(arrived, 0, 1).reshape(occ_col, occ_row, slot_count, square)
    mirror_block = mirror_block.reshape(occ_col, occ_row, slot_count, tile_width, tile_width)
    mine_first = lax.dynamic_index_in_dim(tile_first, my_row, 0, keepdims=False)
    mine_second = lax.dynamic_index_in_dim(tile_second, my_row, 0, keepdims=False)
    their_first = lax.dynamic_index_in_dim(tile_first, partner_row, 0, keepdims=False)
    their_second = lax.dynamic_index_in_dim(tile_second, partner_row, 0, keepdims=False)
    pair_match = (
        (mine_first[:, None] == their_second[None, :])
        & (mine_second[:, None] == their_first[None, :])
    ).astype(jnp.bfloat16)
    crossed = jnp.einsum(
        "st,jitba->ijsab", pair_match, mirror_block, preferred_element_type=jnp.float32
    )
    own_part = cycle_value.astype(jnp.float32)
    symmetric = (own_part + crossed) * live_slots[None, None, :, None, None]
    return symmetric.reshape(occ_row, occ_col, slot_count, square)


def solution(mesh):
    return jax.shard_map(
        on_device,
        mesh=mesh,
        in_specs=(P("row", "col", None, None), P("row", "col", None, None), P(), P()),
        out_specs=P("row", "col", None, None),
        check_vma=False,
    )
```

profile of v0, /device:TPU:3, one launch (start us, length us, event | category | flops | bytes accessed | tf_op | source)
XLA Modules:
  0.0 234.9 jit_solution(8737630853103244513)
XLA Ops:
  6.5 0.0 copy-start
  6.5 0.0 all-gather.2.cloned.1.call-start
  6.5 2.8 %copy.23 = bf16[4,2,12,4096]{3,0,2,1:T(4,128)(2,1)} copy(bf16[4,2,12,4096]{3,1,2,0:T(2,128)(2,1)} %param.4) | data formatting | bytes 1572864 | tf_op args[0]
  9.3 0.0 all-gather.2.cloned.1.call-update
  9.3 0.8 fusion.33
  10.1 0.1 reshape_squeeze.6
  10.2 0.0 copy-done
  10.2 8.5 %gather_fusion = bf16[48,4,2,4096]{3,2,1,0:T(2,128)(2,1)} fusion(bf16[4,2,47,4096]{3,1,2,0:T(2,128)(2,1)S(1)} %copy-done, s32[1024]{0:T(1024)S(1)} %pad_clamp_fusion.1), kind=kCustom, calls=%fused_computation | custom fusion | bytes 6291648 | tf_op jit(solution)/shard_map/jit(_take)/gather | solution.py:30
  18.7 6.6 %broadcast_select_fusion = bf16[4,2,4,12,4096]{4,1,3,0,2:T(2,128)(2,1)} fusion(pred[4,12]{1,0:T(4,128)(4,1)S(1)} %compare_and_fusion.1, bf16[4,2,4,12,4096]{4,1,0,3,2:T(2,128)(2,1)} %bitcast.73), kind=kLoop, calls=%fused_computation.5 | loop fusion | flops 1572864 | bytes 6291504 | tf_op jit(solution)/shard_map/jit(_take)/select_n | solution.py:30
  25.4 0.0 copy-start.4
  25.4 5.0 %all-to-all-start = ((bf16[4,2,4,12,4096]{4,1,3,0,2:T(2,128)(2,1)}), bf16[4,2,4,12,4096]{4,1,3,0,2:T(2,128)(2,1)}, u32[]{:S(2)}, u32[]{:S(2)}) async-start(bf16[4,2,4,12,4096]{4,1,3,0,2:T(2,128)(2,1)} %broadcast_select_fusion), calls=%async_computation | async-start | bytes 6291456 | tf_op jit(solution)/shard_map/all_to_all | solution.py:32
  30.4 0.0 copy-done.4
  30.4 0.6 dynamic_slice.24
  31.0 0.6 compare_convert_fusion
  31.7 69.0 %all-to-all-done = bf16[4,2,4,12,4096]{4,1,3,0,2:T(2,128)(2,1)} async-done(((bf16[4,2,4,12,4096]{4,1,3,0,2:T(2,128)(2,1)}), bf16[4,2,4,12,4096]{4,1,3,0,2:T(2,128)(2,1)}, u32[]{:S(2)}, u32[]{:S(2)}) %all-to-all-start) | async-done | bytes 3145760 | tf_op jit(solution)/shard_map/all_to_all | solution.py:32
  100.6 11.1 %reshape_reshape.9 = bf16[16,2,12,64,64]{4,3,1,2,0:T(8,128)(2,1)} reshape(bf16[4,4,2,1,12,4096]{5,2,4,1,0,3:T(2,128)(2,1)} %bitcast.5) | data formatting | bytes 6291456 | tf_op jit(solution)/shard_map/reshape;reshape | solution.py:37
  111.7 0.0 all-gather.2.cloned.1.call-done
  111.7 9.3 %copy.24 = bf16[4,16,12,4096]{3,1,0,2:T(8,128)(2,1)} copy(bf16[4,16,12,4096]{3,0,2,1:T(4,128)(2,1)} %all-gather.2.cloned.1.call-done) | data formatting | bytes 12582912 | tf_op jit(solution)/shard_map/all_gather | solution.py:34
  121.1 17.9 %reshape.123 = bf16[4,16,12,64,64,1]{4,3,1,0,2,5:T(8,128)(2,1)} reshape(bf16[4,16,12,4096]{3,1,0,2:T(8,128)(2,1)} %copy.24) | data formatting | bytes 12582912 | tf_op jit(solution)/shard_map/reshape | solution.py:36
  139.0 11.1 %fusion.11 = bf16[4,2,12,64,64]{3,4,0,1,2:T(8,128)(2,1)S(1)} fusion(f32[12]{0:T(128)S(1)} %compare_convert_fusion, bf16[4,16,12,64,64,1]{4,3,1,0,2,5:T(8,128)(2,1)} %reshape.123, bf16[16,2,12,64,64]{4,3,1,2,0:T(8,128)(2,1)} %reshape_reshape.9), kind=kOutput, calls=%fused_computation.13 | convolution fusion | flops 806092800 | bytes 10223664 | tf_op jit(solution)/shard_map/iksac,kjscb->ijsab/dot_general | solution.py:38
  150.1 0.0 copy-start.2
  150.1 1.7 copy.26
  151.8 3.1 %reshape_reshape.10 = bf16[2,2,2,12,4096]{4,2,3,1,0:T(2,128)(2,1)S(1)} reshape(bf16[4,2,12,64,64]{4,3,1,2,0:T(8,128)(2,1)} %copy.26) | data formatting | bytes 1572864 | tf_op jit(solution)/shard_map/reshape;reshape | solution.py:45
  154.9 0.8 dynamic-slice_bitcast_fusion.1
  155.7 0.0 copy-done.2
  155.7 0.1 collective-permute-start.1
  155.8 5.8 %collective-permute-start = (bf16[2,2,12,4096]{3,1,2,0:T(2,128)(2,1)S(1)}, bf16[2,2,12,4096]{3,1,2,0:T(2,128)(2,1)S(1)}, u32[]{:S(2)}, u32[]{:S(2)}) collective-permute-start(bf16[2,2,12,4096]{3,1,2,0:T(2,128)(2,1)S(1)} %get-tuple-element.5), channel_id=1, source_target_pairs={{0,0},{1,1},{2,8},{3,9},{4,16},{5,17},{6,24},{7,25},{8,2},{9,3},{1... | collective-permute-start | bytes 1179656 | tf_op jit(solution)/shard_map/ppermute | solution.py:52
  161.7 39.6 %collective-permute-done.1 = bf16[2,2,12,4096]{3,1,2,0:T(2,128)(2,1)S(1)} collective-permute-done((bf16[2,2,12,4096]{3,1,2,0:T(2,128)(2,1)S(1)}, bf16[2,2,12,4096]{3,1,2,0:T(2,128)(2,1)S(1)}, u32[]{:S(2)}, u32[]{:S(2)}) %collective-permute-start.1) | collective-permute-done | bytes 393248 | tf_op jit(solution)/shard_map/ppermute | solution.py:52
  201.3 8.9 %collective-permute-done = bf16[2,2,12,4096]{3,1,2,0:T(2,128)(2,1)S(1)} collective-permute-done((bf16[2,2,12,4096]{3,1,2,0:T(2,128)(2,1)S(1)}, bf16[2,2,12,4096]{3,1,2,0:T(2,128)(2,1)S(1)}, u32[]{:S(2)}, u32[]{:S(2)}) %collective-permute-start) | collective-permute-done | bytes 393248 | tf_op jit(solution)/shard_map/ppermute | solution.py:52
  210.2 1.1 pad_maximum_fusion
  211.4 2.1 gather_fusion.1
  213.5 0.7 fusion.16
  214.2 0.8 copy.27
  215.0 1.0 reshape_reshape.11
  216.1 0.0 copy-start.3
  216.1 1.1 fusion.5
  217.2 0.3 copy-done.3
  217.5 2.7 %fusion.3 = f32[4,2,12,64,64]{3,4,0,1,2:T(8,128)} fusion(f32[2,4,64,64,12]{3,4,2,1,0:T(8,128)S(1)} %fusion.5, bf16[4,2,12,64,64]{3,4,0,1,2:T(8,128)(2,1)S(1)} %copy-done.3, f32[12]{0:T(128)S(1)} %compare_convert_fusion), kind=kLoop, calls=%fused_computation.7 | loop fusion | flops 1179648 | bytes 3932208 | tf_op jit(solution)/shard_map/mul | solution.py:71
  220.2 0.0 copy-start.1
  220.2 3.7 %copy.30 = f32[4,2,12,64,64]{4,3,1,2,0:T(8,128)} copy(f32[4,2,12,64,64]{3,4,0,1,2:T(8,128)} %fusion.3) | data formatting | bytes 3145728 | tf_op jit(solution)/shard_map/mul | solution.py:71
  223.9 4.2 %reshape.105 = f32[4,2,12,4096]{3,1,2,0:T(2,128)} reshape(f32[4,2,12,64,64]{4,3,1,2,0:T(8,128)} %copy.30) | data formatting | bytes 3145728 | tf_op jit(solution)/shard_map/reshape | solution.py:72
  228.1 0.0 copy-done.1
  (7 shorter events, 0.1 us)
Async XLA Ops:
  6.5 3.7 %copy-start = (bf16[4,2,47,4096]{3,1,2,0:T(2,128)(2,1)S(1)}, bf16[4,2,47,4096]{3,1,2,0:T(2,128)(2,1)}, u32[]{:S(2)}) copy-start(bf16[4,2,47,4096]{3,1,2,0:T(2,128)(2,1)} %param.5) | copy-start | bytes 9240580
  6.5 105.2 %all-gather.2.cloned.1.call-start = ((), (), s32[]{:S(2)}) async-start(), calls=%async_computation.1 | async-start | bytes 7077888 | tf_op jit(solution)/shard_map/all_gather | solution.py:34
  25.4 5.0 %copy-start.4 = (s32[4]{0:T(128)S(1)}, s32[4]{0:T(128)}, u32[]{:S(2)}) copy-start(s32[4]{0:T(128)} %param.7) | copy-start | bytes 52
  25.4 75.3 %all-to-all-start = ((bf16[4,2,4,12,4096]{4,1,3,0,2:T(2,128)(2,1)}), bf16[4,2,4,12,4096]{4,1,3,0,2:T(2,128)(2,1)}, u32[]{:S(2)}, u32[]{:S(2)}) async-start(bf16[4,2,4,12,4096]{4,1,3,0,2:T(2,128)(2,1)} %broadcast_select_fusion), calls=%async_computation | async-start | bytes 6291456 | tf_op jit(solution)/shard_map/all_to_all | solution.py:32
  150.1 5.6 %copy-start.2 = (bf16[4,2,12,64,64]{3,4,0,1,2:T(8,128)(2,1)}, bf16[4,2,12,64,64]{3,4,0,1,2:T(8,128)(2,1)S(1)}, u32[]{:S(2)}) copy-start(bf16[4,2,12,64,64]{3,4,0,1,2:T(8,128)(2,1)S(1)} %fusion.11) | copy-start | bytes 2359300
  155.7 45.6 %collective-permute-start.1 = (bf16[2,2,12,4096]{3,1,2,0:T(2,128)(2,1)S(1)}, bf16[2,2,12,4096]{3,1,2,0:T(2,128)(2,1)S(1)}, u32[]{:S(2)}, u32[]{:S(2)}) collective-permute-start(bf16[2,2,12,4096]{3,1,2,0:T(2,128)(2,1)S(1)} %get-tuple-element.6), channel_id=1, source_target_pairs={{0,1},{1,0},{2,9},{3,8},{4,17},{5,16},{6,25},{7,24},{8,3},{9,2},{1... | collective-permute-start | bytes 1179656 | tf_op jit(solution)/shard_map/ppermute | solution.py:52
  155.8 54.4 %collective-permute-start = (bf16[2,2,12,4096]{3,1,2,0:T(2,128)(2,1)S(1)}, bf16[2,2,12,4096]{3,1,2,0:T(2,128)(2,1)S(1)}, u32[]{:S(2)}, u32[]{:S(2)}) collective-permute-start(bf16[2,2,12,4096]{3,1,2,0:T(2,128)(2,1)S(1)} %get-tuple-element.5), channel_id=1, source_target_pairs={{0,0},{1,1},{2,8},{3,9},{4,16},{5,17},{6,24},{7,25},{8,2},{9,3},{1... | collective-permute-start | bytes 1179656 | tf_op jit(solution)/shard_map/ppermute | solution.py:52
  216.1 1.4 copy-start.3
  220.2 7.9 %copy-start.1 = (bf16[4,2,47,4096]{3,1,2,0:T(2,128)(2,1)S(1)}, bf16[4,2,47,4096]{3,1,2,0:T(2,128)(2,1)}, u32[]{:S(2)}) copy-start(bf16[4,2,47,4096]{3,1,2,0:T(2,128)(2,1)} %param.5) | copy-start | bytes 9240580
Sparse Core Ops, SparseCore 0:
  9.5 47.0 all-gather.1
where the time goes:
time: 236 us; the launch traced here: 235 us
  waiting for transfers between devices  118 us (50%)
  local copies, waits for them, and re-layouts  68.9 us (29%)
  between operations  13.6 us (6%)
  matrix products  12.2 us (5%)
  other arithmetic  11.9 us (5%)
  starting transfers between devices  10.9 us (5%)
    all_to_all x1, waiting for transfers between devices, on_device(): lax.all_to_all(packed, 'row', split_axis=2, concat_axis=0, tiled=True)  69 us
    ppermute x2, waiting for transfers between devices, on_device(): lax.ppermute(block, ('row', 'col'), mirror_pairs(row_devices, col_devices...  48.5 us
    reshape x1, local copies, waits for them, and re-layouts, on_device(): piece.reshape(occ_row, piece_count, slot_count, tile_width, tile_width)  17.9 us
    another operation x1, local copies, waits for them, and re-layouts, on_device(): received.reshape(piece_count, occ_col, slot_count, tile_width, tile_width)  11.1 us
    dot_general x1, matrix products, on_device(): jnp.einsum('iksac,kjscb->ijsab', left_tiles, right_tiles, preferred_eleme...  11.1 us
    all_gather x1, local copies, waits for them, and re-layouts, on_device(): piece = lax.all_gather(amplitudes, 'col', axis=1, tiled=True)  9.34 us
    gather x1, local copies, waits for them, and re-layouts, on_device(): packed = jnp.take(integrals, tile_second.reshape(-1), axis=2)  8.51 us
    select_n x2, other arithmetic, on_device(): packed = jnp.take(integrals, tile_second.reshape(-1), axis=2)  6.63 us
  transfers between devices with their start and end apart: 4, of which 3 were waited for; matrix products, arithmetic and copies ran while one was open for 12% of the time, Pallas kernels for 0%

commit v1 on v0

--- a/solution.py
+++ b/solution.py
@@ -2,8 +2,22 @@
 import jax.numpy as jnp
 from jax import lax
 from jax.sharding import PartitionSpec as P
+from jax.lax import axis_index, axis_size, ppermute
 
 TILE = 64
+
+
+def _pass_inputs(s0, which_dim, z_in):
+    work_now, part_next = (s0.shape[:which_dim], s0.shape[which_dim + 1 :])
+    return jnp.moveaxis(s0.reshape(*work_now, z_in, -1, *part_next), which_dim, 0)
+
+
+def extend_rails(local_block, row_dim):
+    local_block = jnp.moveaxis(local_block, 0, row_dim)
+    y_new = local_block.shape
+    return local_block.reshape(
+        *y_new[:row_dim], y_new[row_dim] * y_new[row_dim + 1], *y_new[row_dim + 2 :]
+    )
 
 
 def mirror_pairs(row_devices, col_devices, step):
@@ -29,7 +43,17 @@
     tile_second = pair_lists[:, :, 1]
     packed = jnp.take(integrals, tile_second.reshape(-1), axis=2)
     packed = packed.reshape(occ_row, occ_col, row_devices, slot_count, square)
-    received = lax.all_to_all(packed, "row", split_axis=2, concat_axis=0, tiled=True)
+    outer = axis_size("row")
+    mat_out, x_new = (outer, axis_index("row"))
+    left_arr = _pass_inputs(packed, 2, mat_out)
+    xs_all = [left_arr[x_new]]
+    for ii in tuple(range(1, mat_out)):
+        n_now = left_arr[x_new ^ ii]
+        tmp = ppermute(n_now, "row", [(no, no ^ ii) for no in range(mat_out)])
+        xs_all.append(tmp)
+    r2 = jnp.stack(xs_all, axis=0)
+    left_arr = r2[x_new ^ jnp.arange(mat_out)]
+    received = extend_rails(left_arr, 0)
     received = received.reshape(occ_row * row_devices, occ_col, slot_count, square)
     piece = lax.all_gather(amplitudes, "col", axis=1, tiled=True)
     piece_count = piece.shape[1]

time: 236 us -> 252 us (1.068)
  local copies, waits for them, and re-layouts: 68.9 us -> 85.2 us
  other arithmetic: 11.9 us -> 16.7 us
  waiting for transfers between devices: 118 us -> 115 us
    all_to_all x1 -> x0, waiting for transfers between devices: 69 us -> none  [on_device(): lax.all_to_all(packed, 'row', split_axis=2, concat_axis=0, tiled=True)]
    ppermute x0 -> x3, waiting for transfers between devices: none -> 65.7 us  [on_device(): tmp = ppermute(n_now, 'row', [(no, no ^ ii) for no in range(mat_out)])]
    gather x0 -> x2, local copies, waits for them, and re-layouts: none -> 13.5 us  [on_device(): left_arr = r2[x_new ^ jnp.arange(mat_out)]]
    another operation x0 -> x1, other arithmetic: none -> 5.08 us  [on_device(): r2 = jnp.stack(xs_all, axis=0)]
    all_to_all x1 -> x0, starting transfers between devices: 4.97 us -> none  [on_device(): lax.all_to_all(packed, 'row', split_axis=2, concat_axis=0, tiled=True)]
    ppermute x0 -> x3, starting transfers between devices: none -> 3.63 us  [on_device(): tmp = ppermute(n_now, 'row', [(no, no ^ ii) for no in range(mat_out)])]
    dynamic_slice x0 -> x1, local copies, waits for them, and re-layouts: none -> 2.58 us  [on_device(): xs_all = [left_arr[x_new]]]
  transfers between devices with their start and end apart: 4 -> 6, of which waited for: 3 -> 4; matrix products, arithmetic and copies ran while one was open for 12% -> 20% of each run, Pallas kernels for 0% -> 0%
where the time goes in v1:
time: 252 us; the launch traced here: 251 us
  waiting for transfers between devices  115 us (46%)
  local copies, waits for them, and re-layouts  85.2 us (34%)
  other arithmetic  16.7 us (7%)
  between operations  13.6 us (5%)
  matrix products  12.2 us (5%)
  starting transfers between devices  9.18 us (4%)
    ppermute x3, waiting for transfers between devices, on_device(): tmp = ppermute(n_now, 'row', [(no, no ^ ii) for no in range(mat_out)])  65.7 us
    ppermute x2, waiting for transfers between devices, on_device(): lax.ppermute(block, ('row', 'col'), mirror_pairs(row_devices, col_devices...  48.9 us
    reshape x1, local copies, waits for them, and re-layouts, on_device(): piece.reshape(occ_row, piece_count, slot_count, tile_width, tile_width)  17.9 us
    gather x2, local copies, waits for them, and re-layouts, on_device(): left_arr = r2[x_new ^ jnp.arange(mat_out)]  13.5 us
    another operation x1, local copies, waits for them, and re-layouts, on_device(): received.reshape(piece_count, occ_col, slot_count, tile_width, tile_width)  11.1 us
    dot_general x1, matrix products, on_device(): jnp.einsum('iksac,kjscb->ijsab', left_tiles, right_tiles, preferred_eleme...  11.1 us
    all_gather x1, local copies, waits for them, and re-layouts, on_device(): piece = lax.all_gather(amplitudes, 'col', axis=1, tiled=True)  9.35 us
    gather x1, local copies, waits for them, and re-layouts, on_device(): packed = jnp.take(integrals, tile_second.reshape(-1), axis=2)  8.51 us
  transfers between devices with their start and end apart: 6, of which 4 were waited for; matrix products, arithmetic and copies ran while one was open for 20% of the time, Pallas kernels for 0%

profile of v1, /device:TPU:3, one launch (start us, length us, event | category | flops | bytes accessed | tf_op | source)
XLA Modules:
  0.0 251.4 jit_solution(1225807522598140988)
XLA Ops:
  6.5 0.0 copy-start
  6.5 0.0 all-gather.2.cloned.1.call-start
  6.5 2.8 %copy.24 = bf16[4,2,12,4096]{3,0,2,1:T(4,128)(2,1)} copy(bf16[4,2,12,4096]{3,1,2,0:T(2,128)(2,1)} %param.4) | data formatting | bytes 1572864 | tf_op args[0]
  9.3 0.0 all-gather.2.cloned.1.call-update
  9.4 0.8 fusion.34
  10.1 0.1 reshape_squeeze.6
  10.2 0.0 copy-done
  10.3 8.5 %gather_fusion = bf16[48,4,2,4096]{3,2,1,0:T(2,128)(2,1)} fusion(bf16[4,2,47,4096]{3,1,2,0:T(2,128)(2,1)S(1)} %copy-done, s32[1024]{0:T(1024)S(1)} %pad_clamp_fusion.2), kind=kCustom, calls=%fused_computation | custom fusion | bytes 6291648 | tf_op jit(solution)/shard_map/jit(_take)/gather | solution.py:44
  18.8 6.4 %copy_select_fusion = bf16[4,2,4,1,12,4096]{5,0,4,1,3,2:T(4,128)(2,1)S(1)} fusion(bf16[4,2,4,1,12,4096]{5,1,0,4,2,3:T(2,128)(2,1)} %bitcast.85, pred[4,12]{1,0:T(4,128)(4,1)S(1)} %compare_and_fusion.1), kind=kLoop, calls=%fused_computation.11 | loop fusion | flops 1572864 | bytes 6291504 | tf_op jit(solution)/shard_map/jit(_take)/select_n | solution.py:44
  25.2 0.0 copy-start.4
  25.2 2.6 %dynamic-slice_bitcast_fusion.3 = (bf16[1,4,2,1,12,4096]{5,1,4,2,0,3:T(4,128)(2,1)S(1)}, bf16[4,2,1,12,4096]{4,0,3,1,2:T(4,128)(2,1)}, bf16[4,2,1,12,4096]{4,0,3,1,2:T(4,128)(2,1)}, bf16[4,2,1,12,4096]{4,0,3,1,2:T(4,128)(2,1)}) fusion(bf16[4,2,4,1,12,4096]{5,0,4,1,3,2:T(4,128)(2,1)S(1)} %copy_select_fusion, s32[]{:T(128)S(6)} %select_n.98, ...), kind=kLoop, calls=%fused_computation.20 | loop fusion | bytes 6291472 | tf_op jit(solution)/shard_map/dynamic_slice | solution.py:49
  27.8 3.3 %collective-permute-start.2 = (bf16[4,2,1,12,4096]{4,0,3,1,2:T(4,128)(2,1)}, bf16[4,2,1,12,4096]{4,0,3,1,2:T(4,128)(2,1)S(1)}, u32[]{:S(2)}, u32[]{:S(2)}) collective-permute-start(bf16[4,2,1,12,4096]{4,0,3,1,2:T(4,128)(2,1)} %get-tuple-element.6), channel_id=1, source_target_pairs={{0,24},{8,16},{16,8},{24,0},{1,25},{9,17},{17,9},{25,1},{2,26},{10... | collective-permute-start | bytes 2359304 | tf_op jit(solution)/shard_map/ppermute | solution.py:52
  31.1 0.0 collective-permute-start.1
  31.1 0.3 collective-permute-start
  31.4 0.0 copy-done.4
  31.4 0.6 dynamic_slice.31
  32.0 0.5 compare_convert_fusion
  32.5 16.0 %collective-permute-done.2 = bf16[4,2,1,12,4096]{4,0,3,1,2:T(4,128)(2,1)S(1)} collective-permute-done((bf16[4,2,1,12,4096]{4,0,3,1,2:T(4,128)(2,1)}, bf16[4,2,1,12,4096]{4,0,3,1,2:T(4,128)(2,1)S(1)}, u32[]{:S(2)}, u32[]{:S(2)}) %collective-permute-start.2) | collective-permute-done | bytes 786464 | tf_op jit(solution)/shard_map/ppermute | solution.py:52
  48.5 49.7 %collective-permute-done.1 = bf16[4,2,1,12,4096]{4,0,3,1,2:T(4,128)(2,1)S(1)} collective-permute-done((bf16[4,2,1,12,4096]{4,0,3,1,2:T(4,128)(2,1)}, bf16[4,2,1,12,4096]{4,0,3,1,2:T(4,128)(2,1)S(1)}, u32[]{:S(2)}, u32[]{:S(2)}) %collective-permute-start.1) | collective-permute-done | bytes 786464 | tf_op jit(solution)/shard_map/ppermute | solution.py:52
  98.2 0.0 collective-permute-done
  98.2 5.1 %maximum_bitcast_fusion = bf16[4,4,2,12,4096]{4,1,3,2,0:T(4,128)(2,1)} fusion(bf16[1,4,2,1,12,4096]{5,1,4,2,0,3:T(4,128)(2,1)S(1)} %bitcast.86, bf16[1,4,2,1,12,4096]{5,1,4,2,0,3:T(4,128)(2,1)S(1)} %bitcast.87, bf16[1,4,2,1,12,4096]{5,1,4,2,0,3:T(4,128)(2,1)} %bitcast.6, bf16[1,4,2,1,12,4096]{5,1,4,2,0,3:T(4,128)(2,1)S(1)} %get-tuple-element.5), kind=kLoop, calls=%fused_computation.6 | loop fusion | flops 4718592 | bytes 6291456 | tf_op jit(solution)/shard_map/stack | solution.py:54
  103.3 6.6 %gather_fusion.1 = bf16[4,4,2,12,4096]{4,1,3,2,0:T(4,128)(2,1)} fusion(bf16[4,4,2,12,4096]{4,1,3,2,0:T(4,128)(2,1)} %maximum_bitcast_fusion, s32[1024]{0:T(1024)S(1)} %pad_clamp_fusion.1), kind=kCustom, calls=%fused_computation.1 | custom fusion | bytes 6291472 | tf_op jit(solution)/shard_map/gather | solution.py:55
  109.9 6.9 %copy.23 = bf16[4,4,2,12,4096]{4,2,3,1,0:T(2,128)(2,1)} copy(bf16[4,4,2,12,4096]{4,1,3,2,0:T(4,128)(2,1)} %gather_fusion.1) | data formatting | bytes 6291456 | tf_op jit(solution)/shard_map/gather | solution.py:55
  116.8 11.1 %reshape_reshape_reshape.3 = bf16[16,2,12,64,64]{4,3,1,2,0:T(8,128)(2,1)} reshape(bf16[4,4,2,12,4096]{4,2,3,1,0:T(2,128)(2,1)} %copy.23) | data formatting | bytes 6291456 | tf_op jit(solution)/shard_map/reshape;reshape;reshape | solution.py:61
  127.9 9.4 %copy.25 = bf16[4,16,12,4096]{3,1,0,2:T(8,128)(2,1)} copy(bf16[4,16,12,4096]{3,0,2,1:T(4,128)(2,1)} %all-gather.2.cloned.1.call-done) | data formatting | bytes 12582912 | tf_op jit(solution)/shard_map/all_gather | solution.py:58
  137.2 17.9 %reshape.166 = bf16[4,16,12,64,64,1]{4,3,1,0,2,5:T(8,128)(2,1)} reshape(bf16[4,16,12,4096]{3,1,0,2:T(8,128)(2,1)} %copy.25) | data formatting | bytes 12582912 | tf_op jit(solution)/shard_map/reshape | solution.py:60
  155.2 11.1 %fusion.11 = bf16[4,2,12,64,64]{3,4,0,1,2:T(8,128)(2,1)S(1)} fusion(f32[12]{0:T(128)S(1)} %compare_convert_fusion, bf16[4,16,12,64,64,1]{4,3,1,0,2,5:T(8,128)(2,1)} %reshape.166, bf16[16,2,12,64,64]{4,3,1,2,0:T(8,128)(2,1)} %reshape_reshape_reshape.3), kind=kOutput, calls=%fused_computation.15 | convolution fusion | flops 806092800 | bytes 10223664 | tf_op jit(solution)/shard_map/iksac,kjscb->ijsab/dot_general | solution.py:62
  166.3 0.0 copy-start.2
  166.3 1.7 copy.27
  168.0 3.1 %reshape_reshape.7 = bf16[2,2,2,12,4096]{4,2,3,1,0:T(2,128)(2,1)S(1)} reshape(bf16[4,2,12,64,64]{4,3,1,2,0:T(8,128)(2,1)} %copy.27) | data formatting | bytes 1572864 | tf_op jit(solution)/shard_map/reshape;reshape | solution.py:69
  171.1 0.8 dynamic-slice_bitcast_fusion.5
  171.9 0.0 copy-done.2
  171.9 0.8 collective-permute-start.4
  172.7 4.8 %collective-permute-start.3 = (bf16[2,2,12,4096]{3,1,2,0:T(2,128)(2,1)S(1)}, bf16[2,2,12,4096]{3,1,2,0:T(2,128)(2,1)S(1)}, u32[]{:S(2)}, u32[]{:S(2)}) collective-permute-start(bf16[2,2,12,4096]{3,1,2,0:T(2,128)(2,1)S(1)} %get-tuple-element.9), channel_id=1, source_target_pairs={{0,0},{1,1},{2,8},{3,9},{4,16},{5,17},{6,24},{7,25},{8,2},{9,3},{1... | collective-permute-start | bytes 1179656 | tf_op jit(solution)/shard_map/ppermute | solution.py:76
  177.6 40.1 %collective-permute-done.4 = bf16[2,2,12,4096]{3,1,2,0:T(2,128)(2,1)S(1)} collective-permute-done((bf16[2,2,12,4096]{3,1,2,0:T(2,128)(2,1)S(1)}, bf16[2,2,12,4096]{3,1,2,0:T(2,128)(2,1)S(1)}, u32[]{:S(2)}, u32[]{:S(2)}) %collective-permute-start.4) | collective-permute-done | bytes 393248 | tf_op jit(solution)/shard_map/ppermute | solution.py:76
  217.7 8.8 %collective-permute-done.3 = bf16[2,2,12,4096]{3,1,2,0:T(2,128)(2,1)S(1)} collective-permute-done((bf16[2,2,12,4096]{3,1,2,0:T(2,128)(2,1)S(1)}, bf16[2,2,12,4096]{3,1,2,0:T(2,128)(2,1)S(1)}, u32[]{:S(2)}, u32[]{:S(2)}) %collective-permute-start.3) | collective-permute-done | bytes 393248 | tf_op jit(solution)/shard_map/ppermute | solution.py:76
  226.4 1.1 pad_maximum_fusion
  227.6 2.1 gather_fusion.2
  229.7 0.7 fusion.16
  230.4 0.8 copy.28
  231.2 1.3 reshape_reshape.8
  232.5 0.0 copy-start.3
  232.5 1.1 fusion.5
  233.6 0.3 copy-done.3
  233.9 2.7 %fusion.3 = f32[4,2,12,64,64]{3,4,0,1,2:T(8,128)} fusion(f32[2,4,64,64,12]{3,4,2,1,0:T(8,128)S(1)} %fusion.5, bf16[4,2,12,64,64]{3,4,0,1,2:T(8,128)(2,1)S(1)} %copy-done.3, f32[12]{0:T(128)S(1)} %compare_convert_fusion), kind=kLoop, calls=%fused_computation.8 | loop fusion | flops 1179648 | bytes 3932208 | tf_op jit(solution)/shard_map/mul | solution.py:95
  236.6 3.7 %copy.31 = f32[4,2,12,64,64]{4,3,1,2,0:T(8,128)} copy(f32[4,2,12,64,64]{3,4,0,1,2:T(8,128)} %fusion.3) | data formatting | bytes 3145728 | tf_op jit(solution)/shard_map/mul | solution.py:95
  240.4 4.2 %reshape.137 = f32[4,2,12,4096]{3,1,2,0:T(2,128)} reshape(f32[4,2,12,64,64]{4,3,1,2,0:T(8,128)} %copy.31) | data formatting | bytes 3145728 | tf_op jit(solution)/shard_map/reshape | solution.py:96
  244.5 0.0 copy-done.1
  (11 shorter events, 0.1 us)
Async XLA Ops:
  6.5 3.7 %copy-start = (bf16[4,2,47,4096]{3,1,2,0:T(2,128)(2,1)S(1)}, bf16[4,2,47,4096]{3,1,2,0:T(2,128)(2,1)}, u32[]{:S(2)}) copy-start(bf16[4,2,47,4096]{3,1,2,0:T(2,128)(2,1)} %param.5) | copy-start | bytes 9240580
  6.5 121.4 %all-gather.2.cloned.1.call-start = ((), (), s32[]{:S(2)}) async-start(), calls=%async_computation | async-start | bytes 7077888 | tf_op jit(solution)/shard_map/all_gather | solution.py:58
  25.2 6.2 %copy-start.4 = (s32[4]{0:T(128)S(1)}, s32[4]{0:T(128)}, u32[]{:S(2)}) copy-start(s32[4]{0:T(128)} %param.7) | copy-start | bytes 52
  27.8 20.7 %collective-permute-start.2 = (bf16[4,2,1,12,4096]{4,0,3,1,2:T(4,128)(2,1)}, bf16[4,2,1,12,4096]{4,0,3,1,2:T(4,128)(2,1)S(1)}, u32[]{:S(2)}, u32[]{:S(2)}) collective-permute-start(bf16[4,2,1,12,4096]{4,0,3,1,2:T(4,128)(2,1)} %get-tuple-element.6), channel_id=1, source_target_pairs={{0,24},{8,16},{16,8},{24,0},{1,25},{9,17},{17,9},{25,1},{2,26},{10... | collective-permute-start | bytes 2359304 | tf_op jit(solution)/shard_map/ppermute | solution.py:52
  31.1 67.1 %collective-permute-start.1 = (bf16[4,2,1,12,4096]{4,0,3,1,2:T(4,128)(2,1)}, bf16[4,2,1,12,4096]{4,0,3,1,2:T(4,128)(2,1)S(1)}, u32[]{:S(2)}, u32[]{:S(2)}) collective-permute-start(bf16[4,2,1,12,4096]{4,0,3,1,2:T(4,128)(2,1)} %get-tuple-element.7), channel_id=1, source_target_pairs={{0,16},{8,24},{16,0},{24,8},{1,17},{9,25},{17,1},{25,9},{2,18},{10... | collective-permute-start | bytes 2359304 | tf_op jit(solution)/shard_map/ppermute | solution.py:52
  31.1 67.1 %collective-permute-start = (bf16[4,2,1,12,4096]{4,0,3,1,2:T(4,128)(2,1)}, bf16[4,2,1,12,4096]{4,0,3,1,2:T(4,128)(2,1)}, u32[]{:S(2)}, u32[]{:S(2)}) collective-permute-start(bf16[4,2,1,12,4096]{4,0,3,1,2:T(4,128)(2,1)} %get-tuple-element.8), channel_id=1, source_target_pairs={{0,8},{8,0},{16,24},{24,16},{1,9},{9,1},{17,25},{25,17},{2,10},{10... | collective-permute-start | bytes 2359304 | tf_op jit(solution)/shard_map/ppermute | solution.py:52
  166.3 5.6 %copy-start.2 = (bf16[4,2,12,64,64]{3,4,0,1,2:T(8,128)(2,1)}, bf16[4,2,12,64,64]{3,4,0,1,2:T(8,128)(2,1)S(1)}, u32[]{:S(2)}) copy-start(bf16[4,2,12,64,64]{3,4,0,1,2:T(8,128)(2,1)S(1)} %fusion.11) | copy-start | bytes 2359300
  171.9 45.7 %collective-permute-start.4 = (bf16[2,2,12,4096]{3,1,2,0:T(2,128)(2,1)S(1)}, bf16[2,2,12,4096]{3,1,2,0:T(2,128)(2,1)S(1)}, u32[]{:S(2)}, u32[]{:S(2)}) collective-permute-start(bf16[2,2,12,4096]{3,1,2,0:T(2,128)(2,1)S(1)} %get-tuple-element.10), channel_id=1, source_target_pairs={{0,1},{1,0},{2,9},{3,8},{4,17},{5,16},{6,25},{7,24},{8,3},{9,2},{1... | collective-permute-start | bytes 1179656 | tf_op jit(solution)/shard_map/ppermute | solution.py:76
  172.7 53.8 %collective-permute-start.3 = (bf16[2,2,12,4096]{3,1,2,0:T(2,128)(2,1)S(1)}, bf16[2,2,12,4096]{3,1,2,0:T(2,128)(2,1)S(1)}, u32[]{:S(2)}, u32[]{:S(2)}) collective-permute-start(bf16[2,2,12,4096]{3,1,2,0:T(2,128)(2,1)S(1)} %get-tuple-element.9), channel_id=1, source_target_pairs={{0,0},{1,1},{2,8},{3,9},{4,16},{5,17},{6,24},{7,25},{8,2},{9,3},{1... | collective-permute-start | bytes 1179656 | tf_op jit(solution)/shard_map/ppermute | solution.py:76
  232.5 1.4 copy-start.3
  236.6 7.9 %copy-start.1 = (bf16[4,2,47,4096]{3,1,2,0:T(2,128)(2,1)S(1)}, bf16[4,2,47,4096]{3,1,2,0:T(2,128)(2,1)}, u32[]{:S(2)}) copy-start(bf16[4,2,47,4096]{3,1,2,0:T(2,128)(2,1)} %param.5) | copy-start | bytes 9240580
Sparse Core Ops, SparseCore 0:
  9.5 47.0 all-gather.1
